TPU v7x, 512 devices: a whole 4x4x16 slice. The times are simulated.
512 devices in a mesh: ctx: 64 (over z_hi, x, y, core), pair: 8 (over z_lo).
Axes of the slice: x: 4, y: 4, z: 16 (z_hi: 2, z_lo: 8; z = z_hi * 8 + z_lo), core: 2. Of those that a mesh axis runs over, the one named last changes fastest.
Arguments:
- tokens: bfloat16 [8, 8192, 1536], P('pair', 'ctx'), may hold values from -24 to 24
- w_query: bfloat16 [1536, 512], P('pair'), may hold values from -0.15625 to 0.15625
- w_key: bfloat16 [1536, 128], P('pair'), may hold values from -0.15625 to 0.15625
- w_value: bfloat16 [1536, 192], P('pair'), may hold values from -0.15625 to 0.15625
- w_out: bfloat16 [768, 1536], P('pair'), may hold values from -0.21875 to 0.21875
- norm_gain: float32 [1536], replicated, may hold values from 0.5 to 1.5
- w_pair: bfloat16 [1536, 256], replicated, may hold values from -0.15625 to 0.15625
- conv_weight: bfloat16 [9, 128, 128], replicated, may hold values from -0.1875 to 0.1875
Outputs:
- seq_out: bfloat16 [8, 8192, 1536], P('pair', 'ctx')
- pair_out: bfloat16 [8, 512, 512, 128], P(None, 'ctx', 'pair')
All inputs are finite; a program needn't handle non-finite values.
Results may differ from a plain program's by a relative error of at most 0.014.
The roundings to bfloat16 on the way count: a program that leaves them out, or rounds other values in their place, can miss the bound.
Values may be sent and summed in bfloat16 or wider, within the bound.
A program may use at most 128 MiB of HBM per device.

v0:
```python
import jax
import jax.numpy as jnp
from jax import lax
from jax.sharding import PartitionSpec as P

H = 4
KEY = 128
VAL = 192
PC = 128
POOL = 16
DILATION_STEP = 2


def with_halo(cells, sides, width):
    for axis, dim in sides:
        count = lax.axis_size(axis)
        ends = count - 1
        head = lax.slice_in_dim(cells, 0, width, axis=dim)
        tail = lax.slice_in_dim(cells, cells.shape[dim] - width, cells.shape[dim], axis=dim)
        cells = jnp.concatenate(
            [
                lax.ppermute(tail, axis, [(i, (i + 1) % count) for i in range(ends)]),
                cells,
                lax.ppermute(head, axis, [((i + 1) % count, i) for i in range(ends)]),
            ],
            axis=dim,
        )
    return cells


def on_device(tokens, w_query, w_key, w_value, w_out, norm_gain, w_pair, conv_weight):
    seq_block, row_count, width = tokens.shape
    flat = tokens.reshape(seq_block * row_count, width)
    pieces = (
        lax.all_gather(w_query, "pair", axis=0, tiled=True),
        lax.all_gather(w_key, "pair", axis=0, tiled=True),
        lax.all_gather(w_value, "pair", axis=0, tiled=True),
    )
    columns = flat
    queries, keys, values = tuple(
        (jnp.dot(columns, piece_item, preferred_element_type=jnp.float32) for piece_item in pieces)
    )
    queries = queries.astype(jnp.bfloat16).reshape(seq_block, row_count, H, KEY)
    keys = keys.astype(jnp.bfloat16).reshape(seq_block, row_count, KEY)
    values = values.astype(jnp.bfloat16).reshape(seq_block, row_count, VAL)
    scaling = KEY ** (-0.5)
    highest = jnp.full((seq_block, H, row_count), -1e30, jnp.float32)
    key_piece = lax.all_gather(keys, "ctx", axis=1, tiled=True)
    value_piece = lax.all_gather(values, "ctx", axis=1, tiled=True)
    scores = (
        jnp.einsum("bqhk,bnk->bhqn", queries, key_piece, preferred_element_type=jnp.float32)
        * scaling
    )
    new_high = jnp.maximum(highest, jnp.max(scores, axis=-1))
    weights = jnp.exp(scores - new_high[..., None])
    totals = jnp.sum(weights, axis=-1)
    accum = jnp.einsum(
        "bhqn,bnv->bhqv",
        weights.astype(jnp.bfloat16),
        value_piece,
        preferred_element_type=jnp.float32,
    )
    running = (new_high, totals, accum)
    highest, totals, accum = running
    mixed = (accum / totals[..., None]).astype(jnp.bfloat16)
    mixed = jnp.transpose(mixed, (0, 2, 1, 3)).reshape(seq_block * row_count, H * VAL)
    columns = mixed
    projected = jnp.dot(
        columns,
        lax.all_gather(w_out, "pair", axis=0, tiled=True),
        preferred_element_type=jnp.float32,
    )
    summed = tokens.astype(jnp.float32) + projected.reshape(seq_block, row_count, width)
    seq_out = summed.astype(jnp.bfloat16)
    pooled = jnp.mean(summed.reshape(seq_block, row_count // POOL, POOL, width), axis=2)
    normed = (
        pooled * lax.rsqrt(jnp.mean(pooled * pooled, axis=-1, keepdims=True) + 1e-06) * norm_gain
    )
    normed = normed.astype(jnp.bfloat16)
    averaged_rows = row_count // POOL
    both = jnp.dot(
        normed.reshape(seq_block * averaged_rows, width), w_pair, preferred_element_type=jnp.float32
    ).astype(jnp.bfloat16)
    both = both.reshape(seq_block, averaged_rows, 2 * PC)
    rowpart = both[:, :, :PC]
    colpart = both[:, :, PC:]
    rows_all = lax.all_gather(rowpart, "pair", axis=0, tiled=True)
    ctx_count = lax.axis_size("ctx")
    pair_count = lax.axis_size("pair")
    map_len = averaged_rows * ctx_count
    column_total = map_len // pair_count
    gathered = lax.all_gather(colpart, ("ctx", "pair"), axis=1, tiled=True)
    gathered = gathered.reshape(seq_block, ctx_count, pair_count, averaged_rows, PC)
    gathered = jnp.transpose(gathered, (2, 0, 1, 3, 4)).reshape(pair_count * seq_block, map_len, PC)
    cols_all = lax.dynamic_slice_in_dim(
        gathered, lax.axis_index("pair") * column_total, column_total, 1
    )
    pairwise_grid = (
        rows_all.astype(jnp.float32)[:, :, None, :] * cols_all.astype(jnp.float32)[:, None, :, :]
    ).astype(jnp.bfloat16)
    padded_map = with_halo(pairwise_grid, (("ctx", 1), ("pair", 2)), DILATION_STEP)
    seq_total = pairwise_grid.shape[0]
    cells = seq_total * averaged_rows * column_total
    total = jnp.zeros((cells, PC), jnp.float32)
    for row_offset in range(3):
        for column_offset in range(3):
            kernel_window = padded_map[
                :,
                row_offset * DILATION_STEP : row_offset * DILATION_STEP + averaged_rows,
                column_offset * DILATION_STEP : column_offset * DILATION_STEP + column_total,
                :,
            ]
            total = total + jnp.dot(
                kernel_window.reshape(cells, PC),
                conv_weight[row_offset * 3 + column_offset],
                preferred_element_type=jnp.float32,
            )
    result = pairwise_grid.astype(jnp.float32) + jax.nn.gelu(
        total.reshape(seq_total, averaged_rows, column_total, PC)
    )
    return (seq_out, result.astype(jnp.bfloat16))


def solution(mesh):
    return jax.shard_map(
        on_device,
        mesh=mesh,
        in_specs=(
            P("pair", "ctx", None),
            P("pair", None),
            P("pair", None),
            P("pair", None),
            P("pair", None),
            P(),
            P(),
            P(),
        ),
        out_specs=(P("pair", "ctx", None), P(None, "ctx", "pair", None)),
        check_vma=False,
    )
```

profile of v0, /device:TPU:31, one launch (start us, length us, event | category | flops | bytes accessed | tf_op | source)
XLA Modules:
  0.0 1519.2 jit_solution(11475428438196550576)
XLA Ops:
  7.2 0.0 all-gather.8.cloned.1.call-start
  7.2 0.7 all-gather.8.cloned.1.call-update
  7.9 0.0 all-gather.14.cloned.1.call-start
  8.0 46.8 %all_gather.24 = bf16[1536,128]{1,0:T(8,128)(2,1)S(1)} all-gather(bf16[192,128]{1,0:T(8,128)(2,1)} %param.10), channel_id=1, replica_groups=mesh['ctx'=64,'pair'=8] {'pair'}, dimensions={0}, use_global_device_ids=true | all-gather | bytes 442368 | tf_op jit(solution)/shard_map/all_gather | solution.py:36
  54.8 1.9 convolution_convert_fusion.2
  56.7 0.0 all-gather.16.cloned.1.call-start
  56.8 45.8 %all_gather.27 = bf16[1536,192]{1,0:T(8,128)(2,1)S(1)} all-gather(bf16[192,192]{1,0:T(8,128)(2,1)} %param.11), channel_id=1, replica_groups=mesh['ctx'=64,'pair'=8] {'pair'}, dimensions={0}, use_global_device_ids=true | all-gather | bytes 663552 | tf_op jit(solution)/shard_map/all_gather | solution.py:37
  102.5 1.0 convolution_convert_fusion.1
  103.6 0.0 all-gather.10.cloned.1.call-start
  103.7 0.5 all-gather.10.cloned.1.call-update
  104.2 0.0 all-gather.12.cloned.1.call-start
  104.3 1.8 fusion.22
  106.1 90.0 %all-gather.14.cloned.1.call-done = bf16[8192,128]{1,0:T(8,128)(2,1)} async-done(((bf16[128,128]{1,0:T(8,128)(2,1)}), bf16[8192,128]{1,0:T(8,128)(2,1)}) %all-gather.14.cloned.1.call-update) | async-done | bytes 2097168 | tf_op jit(solution)/shard_map/all_gather | solution.py:48
  196.1 9.7 bitcast_reduce_fusion
  205.7 8.5 fusion.1
  214.3 109.7 %all-gather.16.cloned.1.call-done = bf16[8192,192]{0,1:T(8,128)(2,1)} async-done(((bf16[128,192]{0,1:T(8,128)(2,1)}), bf16[8192,192]{0,1:T(8,128)(2,1)}) %all-gather.16.cloned.1.call-update) | async-done | bytes 3145744 | tf_op jit(solution)/shard_map/all_gather | solution.py:49
  324.0 9.7 fusion.29
  333.7 50.9 %all-gather.10.cloned.1.call-done = bf16[768,1536]{1,0:T(8,128)(2,1)} async-done(((bf16[96,1536]{1,0:T(8,128)(2,1)}), bf16[768,1536]{1,0:T(8,128)(2,1)}) %all-gather.10.cloned.1.call-update) | async-done | bytes 2359312 | tf_op jit(solution)/shard_map/all_gather | solution.py:70
  384.6 2.9 fusion.66
  387.6 0.1 reduce_sum.28
  387.7 0.1 multiply_reduce_fusion
  387.9 0.2 fusion.23
  388.1 0.6 fusion.65
  388.7 37.2 %all_gather.30 = bf16[8,8,128]{2,1,0:T(8,128)(2,1)S(1)} all-gather(bf16[1,8,128]{2,1,0:T(8,128)(2,1)S(1)} %get-tuple-element.16), channel_id=1, replica_groups=mesh['ctx'=64,'pair'=8] {'pair'}, dimensions={0}, use_global_device_ids=true | all-gather | bytes 18432 | tf_op jit(solution)/shard_map/all_gather | solution.py:87
  425.9 1024.5 %all-gather.12.cloned.1.call-done = bf16[1,4096,128]{2,1,0:T(8,128)(2,1)} async-done(((bf16[1,8,128]{2,1,0:T(8,128)(2,1)}), bf16[1,4096,128]{2,1,0:T(8,128)(2,1)}) %all-gather.12.cloned.1.call-update) | async-done | bytes 1048592 | tf_op jit(solution)/shard_map/all_gather | solution.py:92
  1450.5 1.4 copy.30
  1451.9 0.3 multiply_convert_fusion
  1452.3 16.6 %collective-permute-start = (bf16[8,2,64,128]{3,2,1,0:T(8,128)(2,1)S(1)}, bf16[8,2,64,128]{3,2,1,0:T(8,128)(2,1)S(1)}, u32[]{:S(2)}, u32[]{:S(2)}) collective-permute-start(bf16[8,2,64,128]{3,2,1,0:T(8,128)(2,1)S(1)} %get-tuple-element.14), channel_id=1, source_target_pairs={{0,8},{8,16},{16,24},{24,32},{32,40},{40,48},{48,56},{56,64},{64,7... | collective-permute-start | bytes 786440 | tf_op jit(solution)/shard_map/ppermute | solution.py:22
  1468.9 1.9 collective-permute-start.1
  1470.8 1.4 collective-permute-done
  1472.2 17.6 %collective-permute-done.1 = bf16[8,2,64,128]{3,2,1,0:T(8,128)(2,1)S(1)} collective-permute-done((bf16[8,2,64,128]{3,2,1,0:T(8,128)(2,1)S(1)}, bf16[8,2,64,128]{3,2,1,0:T(8,128)(2,1)S(1)}, u32[]{:S(2)}, u32[]{:S(2)}) %collective-permute-start.1) | collective-permute-done | bytes 262176 | tf_op jit(solution)/shard_map/ppermute | solution.py:24
  1489.8 0.1 pad_maximum_fusion.5
  1489.9 10.3 collective-permute-start.2
  1500.3 1.5 collective-permute-start.3
  1501.7 0.2 pad_maximum_fusion.1
  1501.9 0.4 fusion.47
  1502.3 2.8 collective-permute-done.3
  1505.1 1.0 maximum_maximum_fusion
  1506.0 1.4 fusion.62
  1507.4 0.4 fusion.39
  1507.9 0.4 convolution_add_fusion.6
  1508.3 0.4 convolution_add_fusion.5
  1508.7 0.4 convolution_add_fusion.4
  1509.1 0.4 convolution_add_fusion.3
  1509.6 0.4 convolution_add_fusion.2
  1510.0 0.4 convolution_add_fusion.1
  1510.4 0.4 fusion.8
  1510.9 1.8 fusion.19
  (20 shorter events, 0.2 us)
Async XLA Ops:
  7.2 380.7 %copy-start = (bf16[1536,256]{1,0:T(8,128)(2,1)S(1)}, bf16[1536,256]{1,0:T(8,128)(2,1)}, u32[]{:S(2)}) copy-start(bf16[1536,256]{1,0:T(8,128)(2,1)} %param.14) | copy-start | bytes 2359300
  7.2 95.4 %copy-start.2 = (bf16[1,128,1536]{2,1,0:T(8,128)(2,1)S(1)}, bf16[1,128,1536]{2,1,0:T(8,128)(2,1)}, u32[]{:S(2)}) copy-start(bf16[1,128,1536]{2,1,0:T(8,128)(2,1)} %param.8) | copy-start | bytes 1179652
  7.2 97.1 %all-gather.8.cloned.1.call-start = ((), (), s32[]{:S(2)}) async-start(), calls=%async_computation | async-start | bytes 1769472 | tf_op jit(solution)/shard_map/all_gather | solution.py:35
  7.9 188.1 %all-gather.14.cloned.1.call-start = ((), (), s32[]{:S(2)}) async-start(), calls=%async_computation.3 | async-start | bytes 2129920 | tf_op jit(solution)/shard_map/all_gather | solution.py:48
  56.7 267.3 %all-gather.16.cloned.1.call-start = ((), (), s32[]{:S(2)}) async-start(), calls=%async_computation.4 | async-start | bytes 3194880 | tf_op jit(solution)/shard_map/all_gather | solution.py:49
  103.6 281.0 %all-gather.10.cloned.1.call-start = ((), (), s32[]{:S(2)}) async-start(), calls=%async_computation.1 | async-start | bytes 2654208 | tf_op jit(solution)/shard_map/all_gather | solution.py:70
  104.2 1346.3 %all-gather.12.cloned.1.call-start = ((), (), s32[]{:S(2)}) async-start(), calls=%async_computation.2 | async-start | bytes 1050624 | tf_op jit(solution)/shard_map/all_gather | solution.py:92
  384.6 3.2 copy-start.4
  1452.3 19.9 %collective-permute-start = (bf16[8,2,64,128]{3,2,1,0:T(8,128)(2,1)S(1)}, bf16[8,2,64,128]{3,2,1,0:T(8,128)(2,1)S(1)}, u32[]{:S(2)}, u32[]{:S(2)}) collective-permute-start(bf16[8,2,64,128]{3,2,1,0:T(8,128)(2,1)S(1)} %get-tuple-element.14), channel_id=1, source_target_pairs={{0,8},{8,16},{16,24},{24,32},{32,40},{40,48},{48,56},{56,64},{64,7... | collective-permute-start | bytes 786440 | tf_op jit(solution)/shard_map/ppermute | solution.py:22
  1468.9 20.9 %collective-permute-start.1 = (bf16[8,2,64,128]{3,2,1,0:T(8,128)(2,1)S(1)}, bf16[8,2,64,128]{3,2,1,0:T(8,128)(2,1)S(1)}, u32[]{:S(2)}, u32[]{:S(2)}) collective-permute-start(bf16[8,2,64,128]{3,2,1,0:T(8,128)(2,1)S(1)} %get-tuple-element.15), channel_id=1, source_target_pairs={{8,0},{16,8},{24,16},{32,24},{40,32},{48,40},{56,48},{64,56},{72,6... | collective-permute-start | bytes 786440 | tf_op jit(solution)/shard_map/ppermute | solution.py:24
  1489.9 12.0 copy-start.3
  1489.9 12.4 collective-permute-start.2
  1500.3 4.8 collective-permute-start.3
  1510.4 2.3 copy-start.1
Sparse Core Ops, SparseCore 0:
  10.1 69.5 all-gather.7
  84.7 111.3 all-gather.13
  200.9 123.1 all-gather.15
  325.9 58.6 all-gather.9
  388.8 1061.5 all-gather.11
where the time goes:
time: 1520 us
  waiting for transfers between devices  1300 us (86%)
  blocking collectives  130 us (9%)
  matrix products  31 us (2%)
  starting transfers between devices  30.5 us (2%)
    all_gather x1, waiting for transfers between devices, on_device(): gathered = lax.all_gather(colpart, ('ctx', 'pair'), axis=1, tiled=True)  1020 us
    all_gather x1, waiting for transfers between devices, on_device(): value_piece = lax.all_gather(values, 'ctx', axis=1, tiled=True)  110 us
    all_gather x1, waiting for transfers between devices, on_device(): key_piece = lax.all_gather(keys, 'ctx', axis=1, tiled=True)  90 us
    all_gather x1, waiting for transfers between devices, on_device(): lax.all_gather(w_out, 'pair', axis=0, tiled=True)  50.9 us
    all_gather x1, blocking collectives, on_device(): lax.all_gather(w_key, 'pair', axis=0, tiled=True)  46.8 us
    all_gather x1, blocking collectives, on_device(): lax.all_gather(w_value, 'pair', axis=0, tiled=True)  45.8 us
    all_gather x1, blocking collectives, on_device(): rows_all = lax.all_gather(rowpart, 'pair', axis=0, tiled=True)  37.2 us
  transfers between devices with their start and end apart: 9, of which 7 were waited for; matrix products, arithmetic and copies ran while one was open for 2% of the time, Pallas kernels for 0%

commit v1 on v0

--- a/solution.py
+++ b/solution.py
@@ -89,7 +89,12 @@
     pair_count = lax.axis_size("pair")
     map_len = averaged_rows * ctx_count
     column_total = map_len // pair_count
-    gathered = lax.all_gather(colpart, ("ctx", "pair"), axis=1, tiled=True)
+    gathered = jnp.concatenate(
+        lax.all_to_all(
+            jnp.stack([colpart] * lax.axis_size(("ctx", "pair"))), ("ctx", "pair"), 0, 0
+        ),
+        axis=1,
+    )
     gathered = gathered.reshape(seq_block, ctx_count, pair_count, averaged_rows, PC)
     gathered = jnp.transpose(gathered, (2, 0, 1, 3, 4)).reshape(pair_count * seq_block, map_len, PC)
     cols_all = lax.dynamic_slice_in_dim(

time: 1520 us -> 543 us (0.36)
  waiting for transfers between devices: 1300 us -> 274 us
  blocking collectives: 130 us -> 164 us
    all_gather x1 -> x0, waiting for transfers between devices: 1020 us -> none  [on_device(): gathered = lax.all_gather(colpart, ('ctx', 'pair'), axis=1, tiled=True)]
    all_gather x1, blocking collectives: 37.2 us -> 71.8 us  [on_device(): rows_all = lax.all_gather(rowpart, 'pair', axis=0, tiled=True)]
    all_to_all x0 -> x1, starting transfers between devices: none -> 19.8 us  [on_device(): lax.all_to_all(jnp.stack([colpart] * lax.axis_size(('ctx', 'pair'))), ('c...]
  transfers between devices with their start and end apart: 9 -> 9, of which waited for: 7 -> 6; matrix products, arithmetic and copies ran while one was open for 2% -> 6% of each run, Pallas kernels for 0% -> 0%
where the time goes in v1:
time: 543 us; the launch traced here: 542 us
  waiting for transfers between devices  274 us (50%)
  blocking collectives  164 us (30%)
  starting transfers between devices  44.4 us (8%)
  matrix products  31 us (6%)
  between operations  14 us (3%)
  other arithmetic  12.1 us (2%)
    all_gather x1, waiting for transfers between devices, on_device(): value_piece = lax.all_gather(values, 'ctx', axis=1, tiled=True)  110 us
    all_gather x1, waiting for transfers between devices, on_device(): key_piece = lax.all_gather(keys, 'ctx', axis=1, tiled=True)  90.1 us
    all_gather x1, blocking collectives, on_device(): rows_all = lax.all_gather(rowpart, 'pair', axis=0, tiled=True)  71.8 us
    all_gather x1, waiting for transfers between devices, on_device(): lax.all_gather(w_out, 'pair', axis=0, tiled=True)  50.9 us
    all_gather x1, blocking collectives, on_device(): lax.all_gather(w_key, 'pair', axis=0, tiled=True)  46.8 us
    all_gather x1, blocking collectives, on_device(): lax.all_gather(w_value, 'pair', axis=0, tiled=True)  45.8 us
    ppermute x2, starting transfers between devices, with_halo(): lax.ppermute(tail, axis, [(i, (i + 1) % count) for i in range(ends)])  21.3 us
    ppermute x2, waiting for transfers between devices, with_halo(): lax.ppermute(head, axis, [((i + 1) % count, i) for i in range(ends)])  20.3 us
  transfers between devices with their start and end apart: 9, of which 6 were waited for; matrix products, arithmetic and copies ran while one was open for 6% of the time, Pallas kernels for 0%

profile of v1, /device:TPU:31, one launch (start us, length us, event | category | flops | bytes accessed | tf_op | source)
XLA Modules:
  0.0 542.4 jit_solution(7918311177929019047)
XLA Ops:
  7.2 0.0 all-gather.7.cloned.1.call-start
  7.2 0.7 all-gather.7.cloned.1.call-update
  7.9 0.0 all-gather.11.cloned.1.call-start
  8.0 46.8 %all_gather.21 = bf16[1536,128]{1,0:T(8,128)(2,1)S(1)} all-gather(bf16[192,128]{1,0:T(8,128)(2,1)} %param.10), channel_id=1, replica_groups=mesh['ctx'=64,'pair'=8] {'pair'}, dimensions={0}, use_global_device_ids=true | all-gather | bytes 442368 | tf_op jit(solution)/shard_map/all_gather | solution.py:36
  54.8 1.9 convolution_convert_fusion.2
  56.7 0.0 all-gather.13.cloned.1.call-start
  56.8 45.8 %all_gather.24 = bf16[1536,192]{1,0:T(8,128)(2,1)S(1)} all-gather(bf16[192,192]{1,0:T(8,128)(2,1)} %param.11), channel_id=1, replica_groups=mesh['ctx'=64,'pair'=8] {'pair'}, dimensions={0}, use_global_device_ids=true | all-gather | bytes 663552 | tf_op jit(solution)/shard_map/all_gather | solution.py:37
  102.5 1.0 convolution_convert_fusion.1
  103.6 0.0 all-gather.9.cloned.1.call-start
  103.7 0.5 all-gather.9.cloned.1.call-update
  104.2 0.0 all-gather.7.cloned.1.call-done
  104.2 1.8 fusion.22
  106.0 90.1 %all-gather.11.cloned.1.call-done = bf16[8192,128]{1,0:T(8,128)(2,1)} async-done(((bf16[128,128]{1,0:T(8,128)(2,1)}), bf16[8192,128]{1,0:T(8,128)(2,1)}) %all-gather.11.cloned.1.call-update) | async-done | bytes 2097168 | tf_op jit(solution)/shard_map/all_gather | solution.py:48
  196.1 9.7 %bitcast_reduce_fusion = (f32[4,128]{1,0:T(4,128)S(1)}, f32[8192,128,4]{1,0,2:T(8,128)}) fusion(bf16[16,4,8,128]{3,2,1,0:T(8,128)(2,1)S(1)} %fusion.22, bf16[8192,128]{1,0:T(8,128)(2,1)} %all-gather.11.cloned.1.call-done), kind=kOutput, calls=%fused_computation.1 | convolution fusion | flops 1082129920 | bytes 19007488 | tf_op jit(solution)/shard_map/bqhk,bnk->bhqn/dot_general | solution.py:51
  205.7 8.5 %fusion.1 = f32[4,128]{1,0:T(4,128)S(1)} fusion(f32[8192,128,4]{1,0,2:T(8,128)} %get-tuple-element.19, f32[4,128]{1,0:T(4,128)S(1)} %broadcast_maximum_fusion), kind=kLoop, calls=%fused_computation.3 | loop fusion | flops 12582400 | bytes 16781312 | tf_op jit(solution)/shard_map/reduce_sum | solution.py:56
  214.3 109.7 %all-gather.13.cloned.1.call-done = bf16[8192,192]{0,1:T(8,128)(2,1)} async-done(((bf16[128,192]{0,1:T(8,128)(2,1)}), bf16[8192,192]{0,1:T(8,128)(2,1)}) %all-gather.13.cloned.1.call-update) | async-done | bytes 3145744 | tf_op jit(solution)/shard_map/all_gather | solution.py:49
  324.0 9.7 %fusion.29 = bf16[4,128,192]{1,2,0:T(8,128)(2,1)S(1)} fusion(f32[8192,128,4]{1,0,2:T(8,128)} %get-tuple-element.19, f32[4,128]{1,0:T(4,128)S(1)} %broadcast_maximum_fusion, bf16[8192,192]{0,1:T(8,128)(2,1)} %all-gather.13.cloned.1.call-done, f32[4,128]{1,0:T(4,128)S(1)} %fusion.1), kind=kOutput, calls=%fused_computation.45 | convolution fusion | flops 1623392256 | bytes 20123648 | tf_op jit(solution)/shard_map/bhqn,bnv->bhqv/dot_general | solution.py:57
  333.7 50.9 %all-gather.9.cloned.1.call-done = bf16[768,1536]{1,0:T(8,128)(2,1)} async-done(((bf16[96,1536]{1,0:T(8,128)(2,1)}), bf16[768,1536]{1,0:T(8,128)(2,1)}) %all-gather.9.cloned.1.call-update) | async-done | bytes 2359312 | tf_op jit(solution)/shard_map/all_gather | solution.py:70
  384.6 2.9 fusion.66
  387.6 0.1 reduce_sum.28
  387.7 0.1 multiply_reduce_fusion
  387.9 0.2 fusion.23
  388.1 1.1 stack.2
  389.2 19.8 %all-to-all-start = ((bf16[512,1,8,128]{3,2,1,0:T(8,128)(2,1)}), bf16[512,1,8,128]{3,2,1,0:T(8,128)(2,1)S(1)}, u32[]{:S(2)}, u32[]{:S(2)}) async-start(bf16[512,1,8,128]{3,2,1,0:T(8,128)(2,1)} %stack.2), calls=%async_computation | async-start | bytes 2097152 | tf_op jit(solution)/shard_map/all_to_all | solution.py:93
  409.0 71.8 %all_gather.27 = bf16[8,8,128]{2,1,0:T(8,128)(2,1)S(1)} all-gather(bf16[1,8,128]{2,1,0:T(8,128)(2,1)S(1)} %get-tuple-element.16), channel_id=1, replica_groups=mesh['ctx'=64,'pair'=8] {'pair'}, dimensions={0}, use_global_device_ids=true | all-gather | bytes 18432 | tf_op jit(solution)/shard_map/all_gather | solution.py:87
  480.9 0.2 copy.32
  481.1 0.3 multiply_convert_fusion
  481.4 15.9 %collective-permute-start = (bf16[8,2,64,128]{3,2,1,0:T(8,128)(2,1)S(1)}, bf16[8,2,64,128]{3,2,1,0:T(8,128)(2,1)S(1)}, u32[]{:S(2)}, u32[]{:S(2)}) collective-permute-start(bf16[8,2,64,128]{3,2,1,0:T(8,128)(2,1)S(1)} %get-tuple-element.14), channel_id=1, source_target_pairs={{0,8},{8,16},{16,24},{24,32},{32,40},{40,48},{48,56},{56,64},{64,7... | collective-permute-start | bytes 786440 | tf_op jit(solution)/shard_map/ppermute | solution.py:22
  497.3 1.9 collective-permute-start.1
  499.3 1.4 collective-permute-done
  500.6 17.4 %collective-permute-done.1 = bf16[8,2,64,128]{3,2,1,0:T(8,128)(2,1)S(1)} collective-permute-done((bf16[8,2,64,128]{3,2,1,0:T(8,128)(2,1)S(1)}, bf16[8,2,64,128]{3,2,1,0:T(8,128)(2,1)S(1)}, u32[]{:S(2)}, u32[]{:S(2)}) %collective-permute-start.1) | collective-permute-done | bytes 262176 | tf_op jit(solution)/shard_map/ppermute | solution.py:24
  518.0 0.1 pad_maximum_fusion.5
  518.1 5.4 collective-permute-start.2
  523.5 1.3 collective-permute-start.3
  524.8 0.2 pad_maximum_fusion.1
  525.0 0.4 fusion.47
  525.4 2.9 collective-permute-done.3
  528.3 1.0 maximum_maximum_fusion
  529.3 1.4 fusion.62
  530.7 0.4 fusion.39
  531.1 0.4 convolution_add_fusion.6
  531.5 0.4 convolution_add_fusion.5
  531.9 0.4 convolution_add_fusion.4
  532.4 0.4 convolution_add_fusion.3
  532.8 0.4 convolution_add_fusion.2
  533.2 0.4 convolution_add_fusion.1
  533.7 0.4 fusion.8
  534.1 1.8 fusion.19
  (20 shorter events, 0.2 us)
Async XLA Ops:
  7.2 380.7 %copy-start = (bf16[1536,256]{1,0:T(8,128)(2,1)S(1)}, bf16[1536,256]{1,0:T(8,128)(2,1)}, u32[]{:S(2)}) copy-start(bf16[1536,256]{1,0:T(8,128)(2,1)} %param.14) | copy-start | bytes 2359300
  7.2 95.4 %copy-start.2 = (bf16[1,128,1536]{2,1,0:T(8,128)(2,1)S(1)}, bf16[1,128,1536]{2,1,0:T(8,128)(2,1)}, u32[]{:S(2)}) copy-start(bf16[1,128,1536]{2,1,0:T(8,128)(2,1)} %param.8) | copy-start | bytes 1179652
  7.2 97.0 %all-gather.7.cloned.1.call-start = ((), (), s32[]{:S(2)}) async-start(), calls=%async_computation.1 | async-start | bytes 1769472 | tf_op jit(solution)/shard_map/all_gather | solution.py:35
  7.9 188.1 %all-gather.11.cloned.1.call-start = ((), (), s32[]{:S(2)}) async-start(), calls=%async_computation.3 | async-start | bytes 2129920 | tf_op jit(solution)/shard_map/all_gather | solution.py:48
  56.7 267.3 %all-gather.13.cloned.1.call-start = ((), (), s32[]{:S(2)}) async-start(), calls=%async_computation.4 | async-start | bytes 3194880 | tf_op jit(solution)/shard_map/all_gather | solution.py:49
  103.6 281.0 %all-gather.9.cloned.1.call-start = ((), (), s32[]{:S(2)}) async-start(), calls=%async_computation.2 | async-start | bytes 2654208 | tf_op jit(solution)/shard_map/all_gather | solution.py:70
  384.6 3.2 copy-start.4
  389.2 91.6 %all-to-all-start = ((bf16[512,1,8,128]{3,2,1,0:T(8,128)(2,1)}), bf16[512,1,8,128]{3,2,1,0:T(8,128)(2,1)S(1)}, u32[]{:S(2)}, u32[]{:S(2)}) async-start(bf16[512,1,8,128]{3,2,1,0:T(8,128)(2,1)} %stack.2), calls=%async_computation | async-start | bytes 2097152 | tf_op jit(solution)/shard_map/all_to_all | solution.py:93
  481.4 19.2 %collective-permute-start = (bf16[8,2,64,128]{3,2,1,0:T(8,128)(2,1)S(1)}, bf16[8,2,64,128]{3,2,1,0:T(8,128)(2,1)S(1)}, u32[]{:S(2)}, u32[]{:S(2)}) collective-permute-start(bf16[8,2,64,128]{3,2,1,0:T(8,128)(2,1)S(1)} %get-tuple-element.14), channel_id=1, source_target_pairs={{0,8},{8,16},{16,24},{24,32},{32,40},{40,48},{48,56},{56,64},{64,7... | collective-permute-start | bytes 786440 | tf_op jit(solution)/shard_map/ppermute | solution.py:22
  497.3 20.7 %collective-permute-start.1 = (bf16[8,2,64,128]{3,2,1,0:T(8,128)(2,1)S(1)}, bf16[8,2,64,128]{3,2,1,0:T(8,128)(2,1)S(1)}, u32[]{:S(2)}, u32[]{:S(2)}) collective-permute-start(bf16[8,2,64,128]{3,2,1,0:T(8,128)(2,1)S(1)} %get-tuple-element.15), channel_id=1, source_target_pairs={{8,0},{16,8},{24,16},{32,24},{40,32},{48,40},{56,48},{64,56},{72,6... | collective-permute-start | bytes 786440 | tf_op jit(solution)/shard_map/ppermute | solution.py:24
  518.1 6.9 %copy-start.3 = (bf16[9,128,128]{2,1,0:T(8,128)(2,1)S(1)}, bf16[9,128,128]{2,1,0:T(8,128)(2,1)}, u32[]{:S(2)}) copy-start(bf16[9,128,128]{2,1,0:T(8,128)(2,1)} %param.15) | copy-start | bytes 884740
  518.1 7.3 %collective-permute-start.2 = (bf16[8,12,2,128]{3,2,1,0:T(2,128)(2,1)S(1)}, bf16[8,12,2,128]{3,2,1,0:T(2,128)(2,1)S(1)}, u32[]{:S(2)}, u32[]{:S(2)}) collective-permute-start(bf16[8,12,2,128]{3,2,1,0:T(2,128)(2,1)S(1)} %get-tuple-element.10), channel_id=1, source_target_pairs={{0,1},{1,2},{2,3},{3,4},{4,5},{5,6},{6,7},{8,9},{9,10},{10,11},{11... | collective-permute-start | bytes 147464 | tf_op jit(solution)/shard_map/ppermute | solution.py:22
  523.5 4.8 collective-permute-start.3
  533.6 2.3 copy-start.1
Sparse Core Ops, SparseCore 0:
  10.1 69.5 all-gather.6
  84.7 111.3 all-gather.10
  200.9 123.1 all-gather.12
  325.9 58.6 all-gather.8
